TPU v7x, 768 devices: a whole 4x8x12 slice. The times are simulated.
768 devices in a mesh: ctx: 32 (over y, x), dp: 24 (over z, core).
Axes of the slice: x: 4, y: 8, z: 12, core: 2. Of those that a mesh axis runs over, the one named last changes fastest.
Arguments:
- queries: bfloat16 [24, 2, 2048, 512], P('dp', None, 'ctx'), may hold values from -6 to 6
- key_vectors: bfloat16 [24, 2, 2048, 512], P('dp', None, 'ctx'), may hold values from -6 to 6
- value_vectors: bfloat16 [24, 2, 2048, 1024], P('dp', None, 'ctx'), may hold values from -6 to 6
- out_grad: bfloat16 [24, 2, 2048, 1024], P('dp', None, 'ctx'), may hold values from -6 to 6
- forget_logits: bfloat16 [24, 2, 4, 2048], P('dp', None, None, 'ctx'), may hold values from 0 to 16
- input_logits: bfloat16 [24, 2, 4, 2048], P('dp', None, None, 'ctx'), may hold values from -6 to 6
- norm_gain: bfloat16 [1024], replicated, may hold values from 0.099609375 to 1.8984375
Outputs:
- grad_queries: bfloat16 [24, 2, 2048, 512], P('dp', None, 'ctx')
- grad_keys: bfloat16 [24, 2, 2048, 512], P('dp', None, 'ctx')
- grad_values: bfloat16 [24, 2, 2048, 1024], P('dp', None, 'ctx')
- grad_forget: float32 [24, 2, 4, 2048], P('dp', None, None, 'ctx')
- grad_input: float32 [24, 2, 4, 2048], P('dp', None, None, 'ctx')
- grad_gain: float32 [1024], replicated
All inputs are finite; a program needn't handle non-finite values.
Results may differ from a plain program's by a relative error of at most 0.04.
Values sent between devices are 32-bit elements; how exact they have to be, the bound alone decides.
A program may use at most 128 MiB of HBM per device.

v0:
```python
import jax
import jax.numpy as jnp
from jax import lax
from jax.sharding import PartitionSpec as P


def prefix(part, axis, combine, identity, reverse):
    count = lax.axis_size(axis)
    place = lax.axis_index(axis)
    ahead = count - 1 - place if reverse else place
    gathered = jax.tree.map(lambda a: lax.all_gather(a, axis), part)
    state = jax.tree.map(lambda a, e: jnp.zeros_like(a) + jnp.asarray(e, a.dtype), part, identity)

    def one(hop, state):
        source = count - 1 - hop if reverse else hop
        return combine(
            state, jax.tree.map(lambda a: lax.dynamic_index_in_dim(a, source, 0, False), gathered)
        )

    return lax.fori_loop(0, ahead, one, state)


def multiply(form, left, right):
    return jnp.einsum(form, left, right, preferred_element_type=jnp.float32)


def gate_terms(forget_in, input_in):
    forget_logit = forget_in.astype(jnp.float32)
    cum_log = jnp.cumsum(jax.nn.log_sigmoid(forget_logit), axis=-1)
    fade_total = cum_log[..., -1]
    ingate = jax.nn.sigmoid(input_in.astype(jnp.float32))
    span_len = cum_log.shape[-1]
    row_ids = lax.broadcasted_iota(jnp.int32, (span_len, span_len), 0)
    col_ids = lax.broadcasted_iota(jnp.int32, (span_len, span_len), 1)
    causal = row_ids >= col_ids
    spread = cum_log[..., :, None] - cum_log[..., None, :]
    decay_mat = jnp.where(causal, jnp.exp(jnp.where(causal, spread, 0.0)), 0.0)
    reach_fade = jnp.exp(fade_total[..., None] - cum_log)
    return (forget_logit, ingate, cum_log, fade_total, decay_mat, reach_fade)


def block_write(key_part, value_part, ingate, reach_fade):
    weights = jnp.swapaxes(ingate * reach_fade, -1, -2)[..., None]
    scaled = (value_part.astype(jnp.float32) * weights).astype(jnp.bfloat16)
    return multiply("...shd,...shv->...hdv", key_part, scaled)


def block_read(query_part, key_part, value_part, ingate, cum_log, decay_mat, state_in):
    scores = multiply("...thd,...shd->...hts", query_part, key_part)
    mix_weights = (scores * decay_mat * ingate[..., None, :]).astype(jnp.bfloat16)
    state_b = state_in.astype(jnp.bfloat16)
    early_fade = jnp.swapaxes(jnp.exp(cum_log), -1, -2)[..., None]
    hidden = multiply("...hts,...shv->...thv", mix_weights, value_part) + early_fade * multiply(
        "...thd,...hdv->...thv", query_part, state_b
    )
    return (scores, mix_weights, state_b, hidden, early_fade)


def norm_back(hidden, out_part, gain_rows, early_fade, query_part):
    square = jnp.mean(hidden * hidden, axis=-1, keepdims=True)
    inv_rms = lax.rsqrt(square + 1e-05)
    normed = hidden * inv_rms
    pushed = out_part.astype(jnp.float32) * gain_rows
    center = jnp.mean(pushed * normed, axis=-1, keepdims=True)
    grad_hidden = inv_rms * (pushed - normed * center)
    grad_b = grad_hidden.astype(jnp.bfloat16)
    lifted = (grad_hidden * early_fade).astype(jnp.bfloat16)
    back_write = multiply("...thd,...thv->...hdv", query_part, lifted)
    return (grad_hidden, grad_b, normed, back_write)


def block_grads(
    query_part,
    key_part,
    value_part,
    ingate,
    reach_fade,
    decay_mat,
    early_fade,
    scores,
    mix_weights,
    state_b,
    hidden,
    grad_hidden,
    grad_b,
    later_state,
):
    pushed = multiply("...thv,...shv->...hts", grad_b, value_part)
    attend = (pushed * decay_mat * ingate[..., None, :]).astype(jnp.bfloat16)
    later_b = later_state.astype(jnp.bfloat16)
    weights = jnp.swapaxes(ingate * reach_fade, -1, -2)[..., None]
    carried = multiply("...shv,...hdv->...shd", value_part, later_b)
    grad_q = multiply("...hts,...shd->...thd", attend, key_part) + early_fade * multiply(
        "...thv,...hdv->...thd", grad_b, state_b
    )
    grad_k = multiply("...hts,...thd->...shd", attend, query_part) + weights * carried
    grad_v = multiply("...hts,...thv->...shv", mix_weights, grad_b) + weights * multiply(
        "...shd,...hdv->...shv", key_part, later_b
    )
    own_term = jnp.sum(scores * decay_mat * pushed, axis=-2) + reach_fade * jnp.swapaxes(
        jnp.sum(key_part.astype(jnp.float32) * carried, axis=-1), -1, -2
    )
    grad_in = own_term * ingate * (1.0 - ingate)
    lift_term = jnp.swapaxes(jnp.sum(grad_hidden * hidden, axis=-1), -1, -2) - ingate * own_term
    return (grad_q, grad_k, grad_v, grad_in, lift_term)


def tail_cumsum(values_in):
    return jnp.flip(jnp.cumsum(jnp.flip(values_in, -1), axis=-1), -1)


def affine_join(earlier, later):
    return (earlier[0] * later[0], later[0][..., None, None] * earlier[1] + later[1])


def plain_join(earlier, later):
    return earlier + later


def state_path(outward, homeward, identity):
    before_out = prefix(outward, "ctx", affine_join, identity, False)
    through = affine_join(before_out, outward)
    is_last = lax.axis_index("ctx") == lax.axis_size("ctx") - 1
    seeded = affine_join(through, homeward)
    home_items = jax.tree.map(lambda a, b: jnp.where(is_last, a, b), seeded, homeward)
    before_home = prefix(home_items, "ctx", affine_join, identity, True)
    arriving = jnp.where(is_last, through[1], before_home[1])
    return (before_out[1], arriving)


def sum_path(outward, homeward):
    zeros_like = jnp.zeros_like(outward)
    before_out = prefix(outward, "ctx", plain_join, zeros_like, False)
    through = before_out + outward
    is_last = lax.axis_index("ctx") == lax.axis_size("ctx") - 1
    home_items = jnp.where(is_last, through + homeward, homeward)
    before_home = prefix(home_items, "ctx", plain_join, zeros_like, True)
    arriving = jnp.where(is_last, through, before_home)
    return (before_out, arriving)


def shards(queries, key_vectors, value_vectors, out_grad, forget_logits, input_logits, norm_gain):
    batch_rows, halves, block_len, query_width = queries.shape
    head_count = forget_logits.shape[2]
    q_heads = queries.reshape(batch_rows, halves, block_len, head_count, -1)
    k_heads = key_vectors.reshape(batch_rows, halves, block_len, head_count, -1)
    v_heads = value_vectors.reshape(batch_rows, halves, block_len, head_count, -1)
    g_heads = out_grad.reshape(batch_rows, halves, block_len, head_count, -1)
    gain_rows = norm_gain.astype(jnp.float32).reshape(head_count, -1)
    forget_logit, ingate, cum_log, fade_total, decay_mat, reach_fade = gate_terms(
        forget_logits, input_logits
    )
    writes = block_write(k_heads, v_heads, ingate, reach_fade)
    fade_all = jnp.exp(fade_total)
    affine_identity = (jnp.ones_like(fade_all[:, 0]), jnp.zeros_like(writes[:, 0]))
    first_in, second_in = state_path(
        (fade_all[:, 0], writes[:, 0]), (fade_all[:, 1], writes[:, 1]), affine_identity
    )
    state_in = jnp.stack((first_in, second_in), axis=1)
    scores, mix_weights, state_b, hidden, early_fade = block_read(
        q_heads, k_heads, v_heads, ingate, cum_log, decay_mat, state_in
    )
    grad_hidden, grad_b, normed, back_write = norm_back(
        hidden, g_heads, gain_rows, early_fade, q_heads
    )
    gain_part = jnp.sum(g_heads.astype(jnp.float32) * normed, axis=(0, 1, 2))
    later_second, later_first = state_path(
        (fade_all[:, 1], back_write[:, 1]), (fade_all[:, 0], back_write[:, 0]), affine_identity
    )
    later_state = jnp.stack((later_first, later_second), axis=1)
    grad_q, grad_k, grad_v, grad_in, lift_term = block_grads(
        q_heads,
        k_heads,
        v_heads,
        ingate,
        reach_fade,
        decay_mat,
        early_fade,
        scores,
        mix_weights,
        state_b,
        hidden,
        grad_hidden,
        grad_b,
        later_state,
    )
    tail_sum = tail_cumsum(lift_term)
    sum_second, sum_first = sum_path(tail_sum[:, 1, :, 0], tail_sum[:, 0, :, 0])
    later_sum = jnp.stack((sum_first, sum_second), axis=1)
    grad_forget = (tail_sum + later_sum[..., None]) * jax.nn.sigmoid(-forget_logit)
    grad_gain = lax.psum(gain_part, ("ctx", "dp")).reshape(-1)
    grad_queries = grad_q.astype(jnp.bfloat16).reshape(queries.shape)
    grad_keys = grad_k.astype(jnp.bfloat16).reshape(key_vectors.shape)
    grad_values = grad_v.astype(jnp.bfloat16).reshape(value_vectors.shape)
    return (grad_queries, grad_keys, grad_values, grad_forget, grad_in, grad_gain)


def solution(mesh):
    return jax.shard_map(
        shards,
        mesh=mesh,
        in_specs=(
            P("dp", None, "ctx", None),
            P("dp", None, "ctx", None),
            P("dp", None, "ctx", None),
            P("dp", None, "ctx", None),
            P("dp", None, None, "ctx"),
            P("dp", None, None, "ctx"),
            P(),
        ),
        out_specs=(
            P("dp", None, "ctx", None),
            P("dp", None, "ctx", None),
            P("dp", None, "ctx", None),
            P("dp", None, None, "ctx"),
            P("dp", None, None, "ctx"),
            P(),
        ),
        check_vma=False,
    )
```

profile of v0, /device:TPU:6, one launch (start us, length us, event | category | flops | bytes accessed | tf_op | source)
XLA Modules:
  0.0 886.3 jit_solution(11584008266461957740)
XLA Ops:
  13.6 40.7 %all_gather.45 = f32[32,1,4]{2,1,0:T(1,128)S(1)} all-gather(f32[1,1,4]{2,1,0:T(1,128)S(1)} %get-tuple-element.476), channel_id=1, replica_groups=mesh['ctx'=32,'dp'=24] {'ctx'}, dimensions={0}, use_global_device_ids=true | all-gather | bytes 528 | tf_op jit(solution)/shard_map/all_gather | solution.py:11
  54.4 114.8 %all-gather.14.cloned.1.call-done = f32[32,1,4,128,256]{4,3,2,1,0:T(8,128)} async-done(((f32[1,1,4,128,256]{4,3,2,1,0:T(8,128)}), f32[32,1,4,128,256]{4,3,2,1,0:T(8,128)}) %all-gather.14.cloned.1.call-update) | async-done | bytes 16777232 | tf_op jit(solution)/shard_map/all_gather | solution.py:11
  169.3 3.8 while.74
  169.3 1.2 bitcast_add_fusion.15
  175.7 1.3 reshape.302
  179.0 70.2 %all-gather.6 = f32[32,1,4]{2,1,0:T(1,128)} all-gather(f32[1,1,4]{2,1,0:T(1,128)S(1)} %fusion.47), channel_id=2, replica_groups=mesh['ctx'=32,'dp'=24] {'ctx'}, dimensions={0}, use_global_device_ids=true | all-gather | bytes 528 | tf_op jit(solution)/shard_map/all_gather | solution.py:11
  249.2 107.2 %all-gather.18.cloned.1.call-done = f32[32,4,128,256]{3,2,1,0:T(8,128)} async-done(((f32[1,4,128,256]{3,2,1,0:T(8,128)}), f32[32,4,128,256]{3,2,1,0:T(8,128)}) %all-gather.18.cloned.1.call-update) | async-done | bytes 16777232 | tf_op jit(solution)/shard_map/all_gather | solution.py:11
  356.4 52.2 %while.75 = (s32[]{:T(128)}, f32[1,4,128,256]{3,2,1,0:T(8,128)S(1)}, s32[]{:T(128)}, f32[32,1,4]{2,1,0:T(1,128)}, f32[32,1,4,128,256]{4,3,2,1,0:T(8,128)}, /*index=5*/s32[]{:T(128)}, s32[]{:T(128)}, s32[]{:T(128)}, s32[]{:T(128)}) while((s32[]{:T(128)}, f32[1,4,128,256]{3,2,1,0:T(8,128)S(1)}, s32[]{:T(128)}, f32[32,1,4]{2,1,0:T(1,128)}, ...), condition=%wide.region_4.5_spmd, body=%wide.region_3.4_spmd.sunk | while | flops 262150 | bytes 1573059 | solution.py:20
  410.5 1.6 multiply_reduce_fusion.2
  412.2 1.6 fusion.15
  413.7 1.6 multiply_reduce_fusion
  415.4 1.4 convolution_bitcast_fusion
  417.9 39.2 %all_gather.51 = f32[32,1,4]{2,1,0:T(1,128)S(1)} all-gather(f32[1,1,4]{2,1,0:T(1,128)} %get-tuple-element.473), channel_id=1, replica_groups=mesh['ctx'=32,'dp'=24] {'ctx'}, dimensions={0}, use_global_device_ids=true | all-gather | bytes 528 | tf_op jit(solution)/shard_map/all_gather | solution.py:11
  457.1 111.7 %all-gather.16.cloned.1.call-done = f32[32,1,4,128,256]{4,3,2,1,0:T(8,128)} async-done(((f32[1,1,4,128,256]{4,3,2,1,0:T(8,128)}), f32[32,1,4,128,256]{4,3,2,1,0:T(8,128)}) %all-gather.16.cloned.1.call-update) | async-done | bytes 16777232 | tf_op jit(solution)/shard_map/all_gather | solution.py:11
  568.8 3.8 while.76
  568.9 1.2 bitcast_add_fusion.17
  573.4 1.5 add_select_fusion
  575.9 1.7 reshape.303
  582.6 145.8 %psum.7 = f32[1024]{0:T(1024)} all-reduce(f32[1024]{0:T(1024)S(1)} %bitcast.269), channel_id=1, replica_groups=mesh['ctx'=32,'dp'=24] {'ctx','dp'}, use_global_device_ids=true, to_apply=%region_20.21 | all-reduce | flops 1024 | bytes 8192 | tf_op jit(solution)/shard_map/psum | solution.py:191
  729.5 34.2 %all-gather.7 = f32[32,1,4]{2,1,0:T(1,128)S(1)} all-gather(f32[1,1,4]{2,1,0:T(1,128)S(1)} %fusion.48), channel_id=4, replica_groups=mesh['ctx'=32,'dp'=24] {'ctx'}, dimensions={0}, use_global_device_ids=true | all-gather | bytes 528 | tf_op jit(solution)/shard_map/all_gather | solution.py:11
  763.7 34.9 %while.77 = (s32[]{:T(128)}, f32[1,4,128,256]{3,2,1,0:T(8,128)S(1)}, s32[]{:T(128)}, f32[32,1,4]{2,1,0:T(1,128)S(1)}, f32[32,1,4,128,256]{4,3,2,1,0:T(8,128)}, /*index=5*/s32[]{:T(128)}, s32[]{:T(128)}, s32[]{:T(128)}, s32[]{:T(128)}) while((s32[]{:T(128)}, f32[1,4,128,256]{3,2,1,0:T(8,128)S(1)}, s32[]{:T(128)}, f32[32,1,4]{2,1,0:T(1,128)S(1)}, ...), condition=%wide.region_10.11_spmd, body=%wide.region_9.10_spmd.sunk | while | flops 262150 | bytes 1573059 | solution.py:20
  763.8 1.2 bitcast_add_fusion.18
  766.3 1.2 bitcast_add_fusion.18
  768.7 1.2 bitcast_add_fusion.18
  780.0 1.2 bitcast_add_fusion.18
  799.6 1.3 fusion.22
  800.9 1.4 subtract_multiply_fusion.1
  804.0 36.5 %all-gather.4 = f32[32,1,4,1]{2,3,1,0:T(1,128)S(1)} all-gather(f32[1,1,4,1]{2,3,1,0:T(1,128)S(1)} %copy.114), channel_id=6, replica_groups=mesh['ctx'=32,'dp'=24] {'ctx'}, dimensions={0}, use_global_device_ids=true | all-gather | bytes 528 | tf_op jit(solution)/shard_map/all_gather | solution.py:11
  840.6 32.6 %all-gather.8 = f32[32,1,4]{2,1,0:T(1,128)S(1)} all-gather(f32[1,1,4]{2,1,0:T(1,128)S(1)} %fusion.49), channel_id=7, replica_groups=mesh['ctx'=32,'dp'=24] {'ctx'}, dimensions={0}, use_global_device_ids=true | all-gather | bytes 528 | tf_op jit(solution)/shard_map/all_gather | solution.py:11
  874.3 1.3 fusion.9
  876.3 1.4 fusion.13
  878.4 1.3 divide_multiply_fusion
  (243 shorter events, 113.0 us)
Async XLA Ops:
  7.2 167.4 %copy-start.3 = (bf16[1,2,64,512]{3,2,1,0:T(8,128)(2,1)S(1)}, bf16[1,2,64,512]{3,2,1,0:T(8,128)(2,1)}, u32[]{:S(2)}) copy-start(bf16[1,2,64,512]{3,2,1,0:T(8,128)(2,1)} %param.19) | copy-start | bytes 393220
  7.2 162.0 %all-gather.14.cloned.1.call-start = ((), (), s32[]{:S(2)}) async-start(), calls=%async_computation | async-start | bytes 17301504 | tf_op jit(solution)/shard_map/all_gather | solution.py:11
  8.6 5.0 copy-start.6
  8.6 5.0 copy-start.7
  13.1 343.3 %all-gather.18.cloned.1.call-start = ((), (), s32[]{:S(2)}) async-start(), calls=%async_computation.2 | async-start | bytes 17301504 | tf_op jit(solution)/shard_map/all_gather | solution.py:11
  13.6 160.9 %copy-start.8 = (f32[4]{0:T(128)}, f32[4]{0:T(128)S(1)}, u32[]{:S(2)}) copy-start(f32[4]{0:T(128)S(1)} %get-tuple-element.475) | copy-start | bytes 52
  13.6 160.9 %copy-start.9 = (f32[4]{0:T(128)}, f32[4]{0:T(128)S(1)}, u32[]{:S(2)}) copy-start(f32[4]{0:T(128)S(1)} %get-tuple-element.474) | copy-start | bytes 52
  173.1 1.5 copy-start.5
  174.5 394.3 %all-gather.16.cloned.1.call-start = ((), (), s32[]{:S(2)}) async-start(), calls=%async_computation.1 | async-start | bytes 17301504 | tf_op jit(solution)/shard_map/all_gather | solution.py:11
  174.6 181.7 %copy-start.1 = (bf16[2,64,4,128]{3,2,1,0:T(4,128)(2,1)}, bf16[2,64,4,128]{3,2,1,0:T(4,128)(2,1)S(1)}, u32[]{:S(2)}) copy-start(bf16[2,64,4,128]{3,2,1,0:T(4,128)(2,1)S(1)} %reshape.292) | copy-start | bytes 393220
  177.0 179.4 %copy-start.10 = (pred[64,64]{1,0:T(8,128)(4,1)}, pred[64,64]{1,0:T(8,128)(4,1)S(1)}, u32[]{:S(2)}) copy-start(pred[64,64]{1,0:T(8,128)(4,1)S(1)} %iota_compare_fusion) | copy-start | bytes 12292
  410.5 4.8 copy-start
  417.8 345.8 %all-gather.20.cloned.1.call-start = ((), (), s32[]{:S(2)}) async-start(), calls=%async_computation.3 | async-start | bytes 17301504 | tf_op jit(solution)/shard_map/all_gather | solution.py:11
  572.6 0.5 copy-start.4
  578.4 0.7 copy-start.2
Sparse Core Ops, SparseCore 0:
  13.2 155.9 all-gather.13
  174.6 181.6 all-gather.17
  418.0 150.7 all-gather.15
  576.0 182.5 all-gather.19
where the time goes:
time: 892 us; the launch traced here: 886 us
  blocking collectives  399 us (45%)
  waiting for transfers between devices  334 us (37%)
  other arithmetic  90 us (10%)
  local copies, waits for them, and re-layouts  34.2 us (4%)
  between operations  14.1 us (2%)
  matrix products  11.9 us (1%)
    all_gather x4, waiting for transfers between devices, prefix(): gathered = jax.tree.map(lambda a: lax.all_gather(a, axis), part)  334 us
    all_gather x6, blocking collectives, prefix(): gathered = jax.tree.map(lambda a: lax.all_gather(a, axis), part)  253 us
    psum x1, blocking collectives, shards(): grad_gain = lax.psum(gain_part, ('ctx', 'dp')).reshape(-1)  146 us
    add x62, other arithmetic, affine_join(): later[0][..., None, None] * earlier[1] + later[1]  74.2 us
    mul x62, local copies, waits for them, and re-layouts, affine_join(): later[0][..., None, None] * earlier[1] + later[1]  18.3 us
  transfers between devices with their start and end apart: 4, of which 3 were waited for; matrix products, arithmetic and copies ran while one was open for 1% of the time, Pallas kernels for 0%

commit v1 on v0

v1 whole, which is shorter than its diff:
```python
import functools

import jax
import jax.numpy as jnp
from jax import lax
from jax.experimental import pallas as pl
from jax.experimental.pallas import tpu as pltpu
from jax.sharding import PartitionSpec as P

F32 = jnp.float32
BF16 = jnp.bfloat16
MESH = pl.DeviceIdType.MESH
HEADS = 4
CUM, ING, REACH, EARLY, WEIGHT = range(5)


def dot(left, right, left_dim, right_dim):
    return lax.dot_general(
        left, right, (((left_dim,), (right_dim,)), ((), ())), preferred_element_type=F32
    )


def twice(row):
    return jnp.concatenate([row, row], axis=1)


def kernel(
    rows_y,
    count_dp,
    q_ref,
    k_ref,
    v_ref,
    g_ref,
    f_ref,
    i_ref,
    gain_ref,
    gq_ref,
    gk_ref,
    gv_ref,
    gf_ref,
    gi_ref,
    gg_ref,
    s_kv,
    r_kv,
    s_qg,
    r_qg,
    s_gate,
    r_gate,
    s_fade,
    r_fade,
    cols,
    cum_rows,
    ing_rows,
    fade_blk,
    writes,
    totals,
    slices,
    s_state,
    r_state,
    state_b,
    scores_d,
    decay_i,
    mix_b,
    hidden_s,
    grad_b,
    ghh_cols,
    own_cols,
    s_q,
    r_q,
    s_out,
    r_out,
    s_lift,
    r_lift,
    s_fin,
    r_fin,
    s_g1,
    r_g1,
    s_g2,
    r_g2,
    s_g3,
    r_g3,
    x_ss,
    x_rs,
    y_ss,
    y_rs,
    d_ss,
    d_rs,
):
    me = lax.axis_index("ctx")
    my_dp = lax.axis_index("dp")
    my_x = lax.rem(me, HEADS)
    my_y = lax.div(me, HEADS)
    block = q_ref.shape[2]
    dk = q_ref.shape[3] // HEADS
    dv = v_ref.shape[3] // HEADS
    part = dk // rows_y

    def x_peer(step):
        return lax.rem(my_x + step, HEADS)

    def y_peer(step):
        return lax.rem(my_y + step, rows_y)

    def d_peer(step):
        return lax.rem(my_dp + step, count_dp)

    def to_x(step):
        return {"ctx": my_y * HEADS + x_peer(step)}

    def to_y(step):
        return {"ctx": y_peer(step) * HEADS + my_x}

    def to_d(step):
        return {"dp": d_peer(step)}

    started = []

    def send(src, dst, ss, rs, where):
        copy = pltpu.make_async_remote_copy(
            src_ref=src, dst_ref=dst, send_sem=ss, recv_sem=rs, device_id=where, device_id_type=MESH
        )
        copy.start()
        started.append(copy)
        return copy

    def x_send(kind, source, target):
        return [
            send(source(step), target, x_ss.at[kind, step - 1], x_rs.at[kind, step - 1], to_x(step))
            for step in range(1, HEADS)
        ]

    def y_send(kind, source, target):
        return [
            send(source(step), target, y_ss.at[kind, step - 1], y_rs.at[kind, step - 1], to_y(step))
            for step in range(1, rows_y)
        ]

    def arrive(copies):
        for copy in copies:
            copy.wait_recv()

    barrier = pltpu.get_barrier_semaphore()
    peers = (
        [to_x(s) for s in range(1, HEADS)]
        + [to_y(s) for s in range(1, rows_y)]
        + [to_d(s) for s in range(1, count_dp)]
    )
    for peer in peers:
        pl.semaphore_signal(barrier, inc=1, device_id=peer, device_id_type=MESH)

    lane8 = lax.broadcasted_iota(jnp.int32, (8, 128), 1)
    row8 = lax.broadcasted_iota(jnp.int32, (8, 128), 0)
    forget = jnp.concatenate([f_ref[0, 0], f_ref[0, 1]], axis=0).astype(F32)
    ingate_l = jnp.concatenate([i_ref[0, 0], i_ref[0, 1]], axis=0).astype(F32)
    logsig = -jnp.log1p(jnp.exp(-forget))
    ing_own = 1.0 / (1.0 + jnp.exp(-ingate_l))
    packed = jnp.concatenate([logsig, ing_own], axis=1)
    cum = packed
    hop = 1
    while hop < block:
        cum = cum + jnp.where(
            (lane8 >= hop) & (lane8 < block), pltpu.roll(cum, hop, axis=1), 0.0
        )
        hop *= 2
    s_gate[...] = cum
    r_gate[my_x] = cum

    for leg in range(2):
        for head in range(HEADS):
            s_kv[head, leg, :, :dk] = k_ref[0, leg, :, head * dk : (head + 1) * dk].astype(F32)
            s_kv[head, leg, :, dk:] = v_ref[0, leg, :, head * dv : (head + 1) * dv].astype(F32)

    pl.semaphore_wait(barrier, len(peers))
    gate_in = x_send(0, lambda step: s_gate, r_gate.at[my_x])
    kv_in = [
        x_send(1 + leg, lambda step, leg=leg: s_kv.at[x_peer(step), leg], r_kv.at[my_x, leg])
        for leg in range(2)
    ]
    for leg in range(2):
        r_kv[my_x, leg] = s_kv[my_x, leg]
        for head in range(HEADS):
            s_qg[head, leg, :, :dk] = q_ref[0, leg, :, head * dk : (head + 1) * dk].astype(F32)
            s_qg[head, leg, :, dk:] = g_ref[0, leg, :, head * dv : (head + 1) * dv].astype(F32)
        r_qg[my_x, leg] = s_qg[my_x, leg]

    arrive(gate_in)
    gates = jnp.concatenate(
        [
            r_gate[source, pl.ds(leg * HEADS + my_x, 1), :]
            for leg in range(2)
            for source in range(HEADS)
        ],
        axis=0,
    )
    total_log = gates[:, block - 1 : block]
    ingate = pltpu.roll(gates, block, axis=1)
    reach = jnp.exp(total_log - gates)
    cum_rows[...] = gates
    ing_rows[...] = ingate
    fade_blk[...] = jnp.broadcast_to(jnp.exp(total_log), (8, 128))
    stacked = jnp.concatenate(
        [gates, ingate, reach, jnp.exp(gates), ingate * reach, jnp.zeros((88, 128), F32)], axis=0
    )
    cols[...] = jnp.transpose(stacked)
    leg_sum = [
        jnp.sum(total_log[leg * HEADS : (leg + 1) * HEADS], axis=0, keepdims=True)
        for leg in range(2)
    ]
    row_fade = jnp.exp(jnp.where(row8 == 0, leg_sum[0], leg_sum[1]))
    s_fade[...] = row_fade
    r_fade[my_y] = row_fade
    fade_in = y_send(0, lambda step: s_fade, r_fade.at[my_y])

    def col(kind, index):
        at = kind * 8 + index
        return cols[0:block, at : at + 1]

    def fade_of(index):
        return twice(fade_blk[index : index + 1, :])

    def key_of(leg, source):
        return r_kv[source, leg, :, :dk].astype(BF16)

    def value_of(leg, source):
        return r_kv[source, leg, :, dk:].astype(BF16)

    def query_of(leg, source):
        return r_qg[source, leg, :, :dk].astype(BF16)

    onward = list(range(HEADS))
    order = [[onward, onward[::-1]], [onward[::-1], onward]]

    def send_total(phase, leg):
        path = order[phase][leg]
        total = writes[phase, leg, path[0]]
        for source in path[1:]:
            total = fade_of(leg * HEADS + source) * total + writes[phase, leg, source]
        totals[phase, leg] = total.reshape(rows_y, part, dv)
        slices[phase, leg, my_y] = totals[phase, leg, my_y]
        return y_send(
            3 + 4 * phase + 2 * leg,
            lambda step: totals.at[phase, leg, y_peer(step)],
            slices.at[phase, leg, my_y],
        )

    def scan_rows(phase, leg, path, state):
        for row in path:
            s_state[phase, leg, row] = state
            state = twice(r_fade[row, leg : leg + 1, :]) * state + slices[phase, leg, row]
        r_state[phase, leg, my_y] = s_state[phase, leg, my_y]
        copies = y_send(
            4 + 4 * phase + 2 * leg,
            lambda step: s_state.at[phase, leg, y_peer(step)],
            r_state.at[phase, leg, my_y],
        )
        return state, copies

    slices_in = [[None, None], [None, None]]
    states_in = [[None, None], [None, None]]
    for leg in range(2):
        arrive(kv_in[leg])
        for source in range(HEADS):
            value = r_kv[source, leg, :, dk:]
            scaled = (value * col(WEIGHT, leg * HEADS + source)).astype(BF16)
            writes[0, leg, source] = dot(key_of(leg, source), scaled, 0, 0)
        slices_in[0][leg] = send_total(0, leg)

    qg_in = [
        x_send(3 + leg, lambda step, leg=leg: s_qg.at[x_peer(step), leg], r_qg.at[my_x, leg])
        for leg in range(2)
    ]

    row_id = lax.broadcasted_iota(jnp.int32, (block, block), 0)
    col_id = lax.broadcasted_iota(jnp.int32, (block, block), 1)
    causal = col_id >= row_id

    arrive(fade_in)
    upward = list(range(rows_y))
    zero_state = jnp.zeros((part, dv), F32)
    arrive(slices_in[0][0])
    through, states_in[0][0] = scan_rows(0, 0, upward, zero_state)
    arrive(slices_in[0][1])
    _, states_in[0][1] = scan_rows(0, 1, upward[::-1], through)

    for leg in range(2):
        arrive(qg_in[leg])
        for source in range(HEADS):
            index = leg * HEADS + source
            scores = dot(key_of(leg, source), query_of(leg, source), 1, 1)
            spread = cum_rows[index : index + 1, 0:block] - col(CUM, index)
            decay = jnp.where(causal, jnp.exp(jnp.where(causal, spread, 0.0)), 0.0)
            weighted = scores * decay
            mix = (weighted * col(ING, index)).astype(BF16)
            scores_d[index] = weighted
            decay_i[index] = decay * col(ING, index)
            mix_b[index] = mix
            hidden_s[index] = dot(mix, value_of(leg, source), 0, 0)

    lane_b = lax.broadcasted_iota(jnp.int32, (block, 128), 1)
    gain_all = gain_ref[...].astype(F32)
    head_id = lax.broadcasted_iota(jnp.int32, gain_all.shape, 0)
    gain_row = jnp.sum(jnp.where(head_id == my_x, gain_all, 0.0), axis=0, keepdims=True)
    gain_sum = jnp.zeros((8, dv), F32)
    ghh = jnp.zeros((block, 128), F32)
    for leg in range(2):
        arrive(states_in[0][leg])
        state = r_state[0, leg].reshape(dk, dv)
        for source in order[0][leg]:
            index = leg * HEADS + source
            query = query_of(leg, source)
            early = col(EARLY, index)
            rounded = state.astype(BF16)
            state_b[index] = rounded
            hidden = hidden_s[index] + early * dot(query, rounded, 1, 0)
            inv_rms = lax.rsqrt(jnp.mean(hidden * hidden, axis=1, keepdims=True) + 1e-05)
            normed = hidden * inv_rms
            out_grad = r_qg[source, leg, :, dk:]
            pushed = out_grad * gain_row
            center = jnp.mean(pushed * normed, axis=1, keepdims=True)
            grad_hidden = inv_rms * (pushed - normed * center)
            grad_b[index] = grad_hidden.astype(BF16)
            lifted = (grad_hidden * early).astype(BF16)
            writes[1, leg, source] = dot(query, lifted, 0, 0)
            gain_sum = gain_sum + jnp.sum(
                (out_grad * normed).reshape(block // 8, 8, dv), axis=0
            )
            ghh = jnp.where(
                lane_b == index, jnp.sum(grad_hidden * hidden, axis=1, keepdims=True), ghh
            )
            state = fade_of(index) * state + writes[0, leg, source]
    ghh_cols[...] = ghh
    slices_in[1][1] = send_total(1, 1)
    slices_in[1][0] = send_total(1, 0)
    s_g1[...] = gain_sum
    r_g1[my_y] = gain_sum
    gain1_in = y_send(2, lambda step: s_g1, r_g1.at[my_y])

    own_sum = jnp.zeros((block, 128), F32)
    grad_q_in = [None, None]
    for leg in (1, 0):
        for source in range(HEADS):
            index = leg * HEADS + source
            grad = grad_b[index]
            key = key_of(leg, source)
            pushed_mix = dot(value_of(leg, source), grad, 1, 1)
            attend = (pushed_mix * decay_i[index]).astype(BF16)
            own_sum = jnp.where(
                lane_b == index,
                jnp.sum(scores_d[index] * pushed_mix, axis=1, keepdims=True),
                own_sum,
            )
            s_q[source, leg] = dot(attend, key, 0, 0) + col(EARLY, index) * dot(
                grad, state_b[index], 1, 1
            )
            s_out[source, leg, :, :dk] = dot(attend, query_of(leg, source), 1, 0)
            s_out[source, leg, :, dk:] = dot(mix_b[index], grad, 1, 0)
        r_q[my_x, leg] = s_q[my_x, leg]
        grad_q_in[leg] = x_send(
            5 + leg, lambda step, leg=leg: s_q.at[x_peer(step), leg], r_q.at[my_x, leg]
        )
    own_cols[...] = own_sum

    arrive(slices_in[1][1])
    through, states_in[1][1] = scan_rows(1, 1, upward, zero_state)
    arrive(slices_in[1][0])
    _, states_in[1][0] = scan_rows(1, 0, upward[::-1], through)

    arrive(gain1_in)
    gain_sum = r_g1[0]
    for row in range(1, rows_y):
        gain_sum = gain_sum + r_g1[row]
    gain_sum = jnp.sum(gain_sum, axis=0, keepdims=True)
    gain_sum = jnp.concatenate([gain_sum[:, :128], gain_sum[:, 128:]], axis=0)
    s_g2[...] = gain_sum
    r_g2[my_dp] = gain_sum
    gain2_in = [
        send(s_g2, r_g2.at[my_dp], d_ss.at[step - 1], d_rs.at[step - 1], to_d(step))
        for step in range(1, count_dp)
    ]

    own_sum = own_cols[...]
    out_in = [None, None]
    for leg in (1, 0):
        arrive(states_in[1][leg])
        state = r_state[1, leg].reshape(dk, dv)
        for source in order[1][leg]:
            index = leg * HEADS + source
            rounded = state.astype(BF16)
            weight = col(WEIGHT, index)
            carried = dot(value_of(leg, source), rounded, 1, 1)
            s_out[source, leg, :, :dk] = s_out[source, leg, :, :dk] + weight * carried
            s_out[source, leg, :, dk:] = s_out[source, leg, :, dk:] + weight * dot(
                key_of(leg, source), rounded, 1, 0
            )
            extra = col(REACH, index) * jnp.sum(
                r_kv[source, leg, :, :dk] * carried, axis=1, keepdims=True
            )
            own_sum = jnp.where(lane_b == index, own_sum + extra, own_sum)
            state = fade_of(index) * state + writes[1, leg, source]
        r_out[my_x, leg] = s_out[my_x, leg]
        out_in[leg] = x_send(
            7 + leg, lambda step, leg=leg: s_out.at[x_peer(step), leg], r_out.at[my_x, leg]
        )

    turned = jnp.transpose(jnp.concatenate([own_sum, ghh_cols[...]], axis=0))[0:8]
    ing = ing_rows[...]
    lift = pltpu.roll(turned, block, axis=1) - ing * turned
    tail = jnp.where(lane8 < block, lift, 0.0)
    hop = 1
    while hop < block:
        tail = tail + pltpu.roll(tail, 128 - hop, axis=1) * (lane8 < block - hop).astype(F32)
        hop *= 2
    sums = jnp.broadcast_to(tail[:, 0:1], (8, 128))
    leg_total = [
        jnp.sum(sums[leg * HEADS : (leg + 1) * HEADS], axis=0, keepdims=True) for leg in range(2)
    ]
    tile = jnp.where(row8 == 0, leg_total[0], leg_total[1])
    s_lift[...] = tile
    r_lift[my_y] = tile
    lift_in = y_send(1, lambda step: s_lift, r_lift.at[my_y])

    arrive(gain2_in)
    gain_sum = r_g2[0]
    for row in range(1, count_dp):
        gain_sum = gain_sum + r_g2[row]
    s_g3[...] = gain_sum
    r_g3[my_x] = gain_sum
    gain3_in = x_send(10, lambda step: s_g3, r_g3.at[my_x])

    later_rows = [None] * 8
    zero_row = jnp.zeros((1, 128), F32)
    run = zero_row
    for source in range(HEADS):
        later_rows[HEADS + source] = run
        run = run + sums[HEADS + source : HEADS + source + 1]
    run = zero_row
    for source in reversed(range(HEADS)):
        later_rows[source] = run
        run = run + sums[source : source + 1]
    later = jnp.concatenate(later_rows, axis=0)

    arrive(lift_in)
    after_out = zero_row
    after_home = zero_row
    for row in range(rows_y):
        home = r_lift[row, 1:2, :]
        after_out = after_out + home + jnp.where(row > my_y, r_lift[row, 0:1, :], 0.0)
        after_home = after_home + jnp.where(row < my_y, home, 0.0)
    later = later + jnp.where(row8 < HEADS, after_out, after_home)
    fin = jnp.where(
        lane8 < block,
        turned * ing * (1.0 - ing),
        pltpu.roll(tail + later, block, axis=1),
    )
    s_fin[...] = fin
    r_fin[my_x] = fin
    fin_in = x_send(9, lambda step: s_fin, r_fin.at[my_x])

    for leg in (1, 0):
        arrive(grad_q_in[leg])
        for head in range(HEADS):
            gq_ref[0, leg, :, head * dk : (head + 1) * dk] = r_q[head, leg].astype(BF16)
    for leg in (1, 0):
        arrive(out_in[leg])
        for head in range(HEADS):
            gk_ref[0, leg, :, head * dk : (head + 1) * dk] = r_out[head, leg, :, :dk].astype(BF16)
            gv_ref[0, leg, :, head * dv : (head + 1) * dv] = r_out[head, leg, :, dk:].astype(BF16)
    arrive(gain3_in)
    for head in range(HEADS):
        gg_ref[2 * head : 2 * head + 2, :] = r_g3[head]
    arrive(fin_in)
    for leg in range(2):
        rows = jnp.concatenate(
            [r_fin[head, pl.ds(leg * HEADS + my_x, 1), :] for head in range(HEADS)], axis=0
        )
        slope = 1.0 / (1.0 + jnp.exp(f_ref[0, leg].astype(F32)))
        gi_ref[0, leg] = rows[:, :block]
        gf_ref[0, leg] = rows[:, block:] * slope
    for copy in started:
        copy.wait_send()


def shards(rows_y, count_dp, queries, keys, values, out_grad, forget, inputs, gain):
    block = queries.shape[2]
    dk = queries.shape[3] // HEADS
    dv = values.shape[3] // HEADS
    part = dk // rows_y
    vmem = pltpu.VMEM
    scratch = [
        vmem((HEADS, 2, block, dk + dv), F32),
        vmem((HEADS, 2, block, dk + dv), F32),
        vmem((HEADS, 2, block, dk + dv), F32),
        vmem((HEADS, 2, block, dk + dv), F32),
        vmem((8, 128), F32),
        vmem((HEADS, 8, 128), F32),
        vmem((8, 128), F32),
        vmem((rows_y, 8, 128), F32),
        vmem((128, 128), F32),
        vmem((8, 128), F32),
        vmem((8, 128), F32),
        vmem((8, 128), F32),
        vmem((2, 2, HEADS, dk, dv), F32),
        vmem((2, 2, rows_y, part, dv), F32),
        vmem((2, 2, rows_y, part, dv), F32),
        vmem((2, 2, rows_y, part, dv), F32),
        vmem((2, 2, rows_y, part, dv), F32),
        vmem((8, dk, dv), BF16),
        vmem((8, block, block), F32),
        vmem((8, block, block), F32),
        vmem((8, block, block), BF16),
        vmem((8, block, dv), F32),
        vmem((8, block, dv), BF16),
        vmem((block, 128), F32),
        vmem((block, 128), F32),
        vmem((HEADS, 2, block, dk), F32),
        vmem((HEADS, 2, block, dk), F32),
        vmem((HEADS, 2, block, dk + dv), F32),
        vmem((HEADS, 2, block, dk + dv), F32),
        vmem((8, 128), F32),
        vmem((rows_y, 8, 128), F32),
        vmem((8, 128), F32),
        vmem((HEADS, 8, 128), F32),
        vmem((8, dv), F32),
        vmem((rows_y, 8, dv), F32),
        vmem((2, 128), F32),
        vmem((count_dp, 2, 128), F32),
        vmem((2, 128), F32),
        vmem((HEADS, 2, 128), F32),
        pltpu.SemaphoreType.DMA((11, HEADS - 1)),
        pltpu.SemaphoreType.DMA((11, HEADS - 1)),
        pltpu.SemaphoreType.DMA((11, rows_y - 1)),
        pltpu.SemaphoreType.DMA((11, rows_y - 1)),
        pltpu.SemaphoreType.DMA((max(count_dp - 1, 1),)),
        pltpu.SemaphoreType.DMA((max(count_dp - 1, 1),)),
    ]
    spec = pl.BlockSpec(memory_space=pltpu.VMEM)
    outs = pl.pallas_call(
        functools.partial(kernel, rows_y, count_dp),
        out_shape=(
            jax.ShapeDtypeStruct(queries.shape, BF16),
            jax.ShapeDtypeStruct(keys.shape, BF16),
            jax.ShapeDtypeStruct(values.shape, BF16),
            jax.ShapeDtypeStruct(forget.shape, F32),
            jax.ShapeDtypeStruct(inputs.shape, F32),
            jax.ShapeDtypeStruct((8, 128), F32),
        ),
        in_specs=[spec] * 7,
        out_specs=(spec,) * 6,
        scratch_shapes=scratch,
        compiler_params=pltpu.CompilerParams(
            collective_id=0, has_side_effects=True, vmem_limit_bytes=48 * 1024 * 1024
        ),
        name="mlstm_back",
    )(queries, keys, values, out_grad, forget, inputs, gain.reshape(HEADS, -1))
    return outs[:5] + (outs[5].reshape(-1),)


def solution(mesh):
    return jax.shard_map(
        functools.partial(shards, mesh.shape["ctx"] // HEADS, mesh.shape["dp"]),
        mesh=mesh,
        in_specs=(
            P("dp", None, "ctx", None),
            P("dp", None, "ctx", None),
            P("dp", None, "ctx", None),
            P("dp", None, "ctx", None),
            P("dp", None, None, "ctx"),
            P("dp", None, None, "ctx"),
            P(),
        ),
        out_specs=(
            P("dp", None, "ctx", None),
            P("dp", None, "ctx", None),
            P("dp", None, "ctx", None),
            P("dp", None, None, "ctx"),
            P("dp", None, None, "ctx"),
            P(),
        ),
        check_vma=False,
    )
```

time: 892 us -> 79.9 us (0.09)
  blocking collectives: 399 us -> 0 us
  waiting for transfers between devices: 334 us -> 0 us
  other arithmetic: 90 us -> 0 us
  Pallas kernels: 0 us -> 70.3 us
  local copies, waits for them, and re-layouts: 34.2 us -> 8.2 us
  between operations: 14.1 us -> 0.67 us
  matrix products: 11.9 us -> 0 us
    all_gather x4 -> x0, waiting for transfers between devices: 334 us -> none  [prefix(): gathered = jax.tree.map(lambda a: lax.all_gather(a, axis), part)]
    all_gather x6 -> x0, blocking collectives: 253 us -> none  [prefix(): gathered = jax.tree.map(lambda a: lax.all_gather(a, axis), part)]
    psum x1 -> x0, blocking collectives: 146 us -> none  [shards(): grad_gain = lax.psum(gain_part, ('ctx', 'dp')).reshape(-1)]
    add x94 -> x0, other arithmetic: 74.7 us -> none  [the longest x62 74.2 us: affine_join(): later[0][..., None, None] * earlier[1] + later[1]]
    pallas_call x0 -> x1, Pallas kernels: none -> 70.3 us  [shards(): pl.pallas_call(functools.partial(kernel, rows_y, count_dp), out_shape=(ja...]
    mul x63 -> x0, local copies, waits for them, and re-layouts: 19.6 us -> none  [the longest x62 18.3 us: affine_join(): later[0][..., None, None] * earlier[1] + later[1]]
    dot_general x12 -> x0, matrix products: 11.9 us -> none  [multiply(): return jnp.einsum(form, left, right, preferred_element_type=jnp.float32)]
  transfers between devices with their start and end apart: 4 -> 0, of which waited for: 3 -> 0; matrix products, arithmetic and copies ran while one was open for 1% -> 0% of each run, Pallas kernels for 0% -> 0%
where the time goes in v1:
time: 79.9 us; the launch traced here: 79.2 us
  Pallas kernels  70.3 us (88%)
  local copies, waits for them, and re-layouts  8.2 us (10%)
    pallas_call x1, Pallas kernels, shards(): pl.pallas_call(functools.partial(kernel, rows_y, count_dp), out_shape=(ja...  70.3 us
    unnamed x18, local copies, waits for them, and re-layouts  7.5 us

profile of v1, /device:TPU:6, one launch (start us, length us, event | category | flops | bytes accessed | tf_op | source)
XLA Modules:
  0.0 79.2 jit_solution(13795168976937076224)
XLA Ops:
  0.6 0.0 copy-start.5
  0.6 0.0 copy-start.4
  0.7 0.7 reshape.18.gain_ref
  1.4 0.0 copy-done.5
  1.4 0.0 copy-done.4
  1.4 0.0 copy-start
  1.4 0.9 %copy-done = bf16[1,2,64,1024]{3,2,1,0:T(8,128)(2,1)S(1)} copy-done((bf16[1,2,64,1024]{3,2,1,0:T(8,128)(2,1)S(1)}, bf16[1,2,64,1024]{3,2,1,0:T(8,128)(2,1)}, u32[]{:S(2)}) %copy-start) | copy-done | bytes 262168
  2.3 0.0 copy-start.1
  2.3 0.9 %copy-done.1 = bf16[1,2,64,1024]{3,2,1,0:T(8,128)(2,1)S(1)} copy-done((bf16[1,2,64,1024]{3,2,1,0:T(8,128)(2,1)S(1)}, bf16[1,2,64,1024]{3,2,1,0:T(8,128)(2,1)}, u32[]{:S(2)}) %copy-start.1) | copy-done | bytes 262168
  3.3 0.0 copy-start.2
  3.3 0.9 %copy-done.2 = bf16[1,2,64,512]{3,2,1,0:T(8,128)(2,1)S(1)} copy-done((bf16[1,2,64,512]{3,2,1,0:T(8,128)(2,1)S(1)}, bf16[1,2,64,512]{3,2,1,0:T(8,128)(2,1)}, u32[]{:S(2)}) %copy-start.2) | copy-done | bytes 131096
  4.2 0.0 copy-start.3
  4.2 0.9 %copy-done.3 = bf16[1,2,64,512]{3,2,1,0:T(8,128)(2,1)S(1)} copy-done((bf16[1,2,64,512]{3,2,1,0:T(8,128)(2,1)S(1)}, bf16[1,2,64,512]{3,2,1,0:T(8,128)(2,1)}, u32[]{:S(2)}) %copy-start.3) | copy-done | bytes 131096
  5.1 70.3 %mlstm_back.1 = (bf16[1,2,64,512]{3,2,1,0:T(8,128)(2,1)S(1)}, bf16[1,2,64,512]{3,2,1,0:T(8,128)(2,1)S(1)}, bf16[1,2,64,1024]{3,2,1,0:T(8,128)(2,1)S(1)}, f32[1,2...) custom-call(bf16[1,2,64,512]{3,2,1,0:T(8,128)(2,1)S(1)} %copy-done.2, ...), custom_call_target="tpu_custom_call" | custom-call | tf_op jit(solution)/shard_map/mlstm_back/pallas_call | solution.py:537
  75.4 0.7 copy.19
  76.0 0.7 copy.20
  76.7 0.7 copy.21
  77.4 0.6 copy.22
  78.0 0.6 copy.23
  78.6 0.6 copy.24
Async XLA Ops:
  0.6 0.7 copy-start.5
  0.6 0.7 copy-start.4
  1.4 1.0 %copy-start = (bf16[1,2,64,1024]{3,2,1,0:T(8,128)(2,1)S(1)}, bf16[1,2,64,1024]{3,2,1,0:T(8,128)(2,1)}, u32[]{:S(2)}) copy-start(bf16[1,2,64,1024]{3,2,1,0:T(8,128)(2,1)} %v_ref.1) | copy-start | bytes 786436
  2.3 0.9 %copy-start.1 = (bf16[1,2,64,1024]{3,2,1,0:T(8,128)(2,1)S(1)}, bf16[1,2,64,1024]{3,2,1,0:T(8,128)(2,1)}, u32[]{:S(2)}) copy-start(bf16[1,2,64,1024]{3,2,1,0:T(8,128)(2,1)} %g_ref.1) | copy-start | bytes 786436
  3.3 0.9 %copy-start.2 = (bf16[1,2,64,512]{3,2,1,0:T(8,128)(2,1)S(1)}, bf16[1,2,64,512]{3,2,1,0:T(8,128)(2,1)}, u32[]{:S(2)}) copy-start(bf16[1,2,64,512]{3,2,1,0:T(8,128)(2,1)} %q_ref.1) | copy-start | bytes 393220
  4.2 0.9 %copy-start.3 = (bf16[1,2,64,512]{3,2,1,0:T(8,128)(2,1)S(1)}, bf16[1,2,64,512]{3,2,1,0:T(8,128)(2,1)}, u32[]{:S(2)}) copy-start(bf16[1,2,64,512]{3,2,1,0:T(8,128)(2,1)} %k_ref.1) | copy-start | bytes 393220

commit v2 on v1

--- a/solution.py
+++ b/solution.py
@@ -27,6 +27,19 @@
 def kernel(
     rows_y,
     count_dp,
+    q_hbm,
+    k_hbm,
+    v_hbm,
+    g_hbm,
+    f_hbm,
+    i_hbm,
+    gain_hbm,
+    gq_ref,
+    gk_ref,
+    gv_ref,
+    gf_ref,
+    gi_ref,
+    gg_ref,
     q_ref,
     k_ref,
     v_ref,
@@ -34,12 +47,7 @@
     f_ref,
     i_ref,
     gain_ref,
-    gq_ref,
-    gk_ref,
-    gv_ref,
-    gf_ref,
-    gi_ref,
-    gg_ref,
+    in_sem,
     s_kv,
     r_kv,
     s_qg,
@@ -85,7 +93,28 @@
     y_rs,
     d_ss,
     d_rs,
+    g1_ss,
+    g1_rs,
+    g3_ss,
+    g3_rs,
+    ready,
 ):
+    inputs = [
+        pltpu.make_async_copy(src, dst, in_sem.at[number])
+        for number, (src, dst) in enumerate(
+            [
+                (f_hbm, f_ref),
+                (i_hbm, i_ref),
+                (k_hbm, k_ref),
+                (v_hbm, v_ref),
+                (q_hbm, q_ref),
+                (g_hbm, g_ref),
+                (gain_hbm, gain_ref),
+            ]
+        )
+    ]
+    for copy in inputs:
+        copy.start()
     me = lax.axis_index("ctx")
     my_dp = lax.axis_index("dp")
     my_x = lax.rem(me, HEADS)
@@ -139,17 +168,35 @@
         for copy in copies:
             copy.wait_recv()
 
+    is_gate = my_x == my_y
     barrier = pltpu.get_barrier_semaphore()
-    peers = (
-        [to_x(s) for s in range(1, HEADS)]
-        + [to_y(s) for s in range(1, rows_y)]
-        + [to_d(s) for s in range(1, count_dp)]
-    )
-    for peer in peers:
-        pl.semaphore_signal(barrier, inc=1, device_id=peer, device_id_type=MESH)
+    plane = HEADS - 1 + rows_y - 1
+
+    def signal(sem, where):
+        pl.semaphore_signal(sem, inc=1, device_id=where, device_id_type=MESH)
+
+    for step in range(1, HEADS):
+
+        @pl.when(x_peer(step) != my_y)
+        def _():
+            signal(barrier, to_x(step))
+
+    for step in range(1, rows_y):
+
+        @pl.when(y_peer(step) != my_x)
+        def _():
+            signal(barrier, to_y(step))
+
+    @pl.when(is_gate)
+    def _():
+        for step in range(1, count_dp):
+            signal(barrier, to_d(step))
+
 
     lane8 = lax.broadcasted_iota(jnp.int32, (8, 128), 1)
     row8 = lax.broadcasted_iota(jnp.int32, (8, 128), 0)
+    inputs[0].wait()
+    inputs[1].wait()
     forget = jnp.concatenate([f_ref[0, 0], f_ref[0, 1]], axis=0).astype(F32)
     ingate_l = jnp.concatenate([i_ref[0, 0], i_ref[0, 1]], axis=0).astype(F32)
     logsig = -jnp.log1p(jnp.exp(-forget))
@@ -165,17 +212,36 @@
     s_gate[...] = cum
     r_gate[my_x] = cum
 
+    inputs[2].wait()
+    inputs[3].wait()
     for leg in range(2):
         for head in range(HEADS):
             s_kv[head, leg, :, :dk] = k_ref[0, leg, :, head * dk : (head + 1) * dk].astype(F32)
             s_kv[head, leg, :, dk:] = v_ref[0, leg, :, head * dv : (head + 1) * dv].astype(F32)
 
-    pl.semaphore_wait(barrier, len(peers))
+    @pl.when(jnp.logical_not(is_gate))
+    def _():
+        pl.semaphore_wait(barrier, plane)
+
+        @pl.when((my_y < HEADS) & (my_x == lax.rem(my_y + 1, HEADS)))
+        def _():
+            signal(ready, {"ctx": my_y * HEADS + my_y})
+
+        @pl.when(my_y == lax.rem(my_x + 1, rows_y))
+        def _():
+            signal(ready, {"ctx": my_x * HEADS + my_x})
+
+    @pl.when(is_gate)
+    def _():
+        pl.semaphore_wait(ready, 2)
+
     gate_in = x_send(0, lambda step: s_gate, r_gate.at[my_x])
     kv_in = [
         x_send(1 + leg, lambda step, leg=leg: s_kv.at[x_peer(step), leg], r_kv.at[my_x, leg])
         for leg in range(2)
     ]
+    for copy in inputs[4:]:
+        copy.wait()
     for leg in range(2):
         r_kv[my_x, leg] = s_kv[my_x, leg]
         for head in range(HEADS):
@@ -299,7 +365,13 @@
     lane_b = lax.broadcasted_iota(jnp.int32, (block, 128), 1)
     gain_all = gain_ref[...].astype(F32)
     head_id = lax.broadcasted_iota(jnp.int32, gain_all.shape, 0)
-    gain_row = jnp.sum(jnp.where(head_id == my_x, gain_all, 0.0), axis=0, keepdims=True)
+    gain_row = jnp.concatenate(
+        [
+            jnp.sum(jnp.where(head_id == 2 * my_x + half, gain_all, 0.0), axis=0, keepdims=True)
+            for half in range(2)
+        ],
+        axis=1,
+    )
     gain_sum = jnp.zeros((8, dv), F32)
     ghh = jnp.zeros((block, 128), F32)
     for leg in range(2):
@@ -331,9 +403,30 @@
     ghh_cols[...] = ghh
     slices_in[1][1] = send_total(1, 1)
     slices_in[1][0] = send_total(1, 0)
+    gain_sum = jnp.sum(gain_sum, axis=0, keepdims=True)
+    gain_sum = jnp.concatenate([gain_sum[:, :128], gain_sum[:, 128:]], axis=0)
     s_g1[...] = gain_sum
     r_g1[my_y] = gain_sum
-    gain1_in = y_send(2, lambda step: s_g1, r_g1.at[my_y])
+
+    def remote(src, dst, ss, rs, where):
+        return pltpu.make_async_remote_copy(
+            src_ref=src, dst_ref=dst, send_sem=ss, recv_sem=rs, device_id=where, device_id_type=MESH
+        )
+
+    def gain1():
+        gate = {"ctx": my_x * HEADS + my_x}
+        return remote(s_g1, r_g1.at[my_y], g1_ss.at[0], g1_rs.at[my_y], gate)
+
+    def gain2(step):
+        return remote(s_g2, r_g2.at[my_dp], d_ss.at[step - 1], d_rs.at[step - 1], to_d(step))
+
+    def gain3(step):
+        where = {"ctx": lax.rem(me + step, HEADS * rows_y)}
+        return remote(s_g3, r_g3.at[my_x], g3_ss.at[step - 1], g3_rs.at[my_x], where)
+
+    @pl.when(jnp.logical_not(is_gate))
+    def _():
+        gain1().start()
 
     own_sum = jnp.zeros((block, 128), F32)
     grad_q_in = [None, None]
@@ -365,18 +458,21 @@
     arrive(slices_in[1][0])
     _, states_in[1][0] = scan_rows(1, 0, upward[::-1], through)
 
-    arrive(gain1_in)
-    gain_sum = r_g1[0]
-    for row in range(1, rows_y):
-        gain_sum = gain_sum + r_g1[row]
-    gain_sum = jnp.sum(gain_sum, axis=0, keepdims=True)
-    gain_sum = jnp.concatenate([gain_sum[:, :128], gain_sum[:, 128:]], axis=0)
-    s_g2[...] = gain_sum
-    r_g2[my_dp] = gain_sum
-    gain2_in = [
-        send(s_g2, r_g2.at[my_dp], d_ss.at[step - 1], d_rs.at[step - 1], to_d(step))
-        for step in range(1, count_dp)
-    ]
+    @pl.when(is_gate)
+    def _():
+        for step in range(1, rows_y):
+            row = y_peer(step)
+            remote(s_g1, r_g1.at[row], g1_ss.at[0], g1_rs.at[row], to_y(step)).wait_recv()
+        gain_sum = r_g1[0]
+        for row in range(1, rows_y):
+            gain_sum = gain_sum + r_g1[row]
+        s_g2[...] = gain_sum
+        r_g2[my_dp] = gain_sum
+        if count_dp > 1:
+            pl.semaphore_wait(barrier, count_dp - 1)
+        for step in range(1, count_dp):
+            gain2(step).start()
+
 
     own_sum = own_cols[...]
     out_in = [None, None]
@@ -419,14 +515,6 @@
     r_lift[my_y] = tile
     lift_in = y_send(1, lambda step: s_lift, r_lift.at[my_y])
 
-    arrive(gain2_in)
-    gain_sum = r_g2[0]
-    for row in range(1, count_dp):
-        gain_sum = gain_sum + r_g2[row]
-    s_g3[...] = gain_sum
-    r_g3[my_x] = gain_sum
-    gain3_in = x_send(10, lambda step: s_g3, r_g3.at[my_x])
-
     later_rows = [None] * 8
     zero_row = jnp.zeros((1, 128), F32)
     run = zero_row
@@ -465,9 +553,6 @@
         for head in range(HEADS):
             gk_ref[0, leg, :, head * dk : (head + 1) * dk] = r_out[head, leg, :, :dk].astype(BF16)
             gv_ref[0, leg, :, head * dv : (head + 1) * dv] = r_out[head, leg, :, dk:].astype(BF16)
-    arrive(gain3_in)
-    for head in range(HEADS):
-        gg_ref[2 * head : 2 * head + 2, :] = r_g3[head]
     arrive(fin_in)
     for leg in range(2):
         rows = jnp.concatenate(
@@ -476,8 +561,49 @@
         slope = 1.0 / (1.0 + jnp.exp(f_ref[0, leg].astype(F32)))
         gi_ref[0, leg] = rows[:, :block]
         gf_ref[0, leg] = rows[:, block:] * slope
+
+    @pl.when(is_gate)
+    def _():
+        for step in range(1, count_dp):
+            gain2(step).wait_recv()
+        gain_sum = r_g2[0]
+        for row in range(1, count_dp):
+            gain_sum = gain_sum + r_g2[row]
+        s_g3[...] = gain_sum
+        r_g3[my_x] = gain_sum
+        for step in range(1, HEADS * rows_y):
+            gain3(step).start()
+
     for copy in started:
         copy.wait_send()
+    for head in range(HEADS):
+
+        @pl.when(me != head * HEADS + head)
+        def _():
+            where = {"ctx": head * HEADS + head}
+            remote(s_g3, r_g3.at[head], g3_ss.at[0], g3_rs.at[head], where).wait_recv()
+
+        gg_ref[2 * head : 2 * head + 2, :] = r_g3[head]
+
+    @pl.when(is_gate)
+    def _():
+        for step in range(1, count_dp):
+            gain2(step).wait_send()
+        for step in range(1, HEADS * rows_y):
+            gain3(step).wait_send()
+
+    @pl.when(jnp.logical_not(is_gate))
+    def _():
+        gain1().wait_send()
+
+
+def store(*refs):
+    sems = refs[12]
+    copies = [pltpu.make_async_copy(refs[n], refs[6 + n], sems.at[n]) for n in range(6)]
+    for copy in copies:
+        copy.start()
+    for copy in copies:
+        copy.wait()
 
 
 def shards(rows_y, count_dp, queries, keys, values, out_grad, forget, inputs, gain):
@@ -487,6 +613,14 @@
     part = dk // rows_y
     vmem = pltpu.VMEM
     scratch = [
+        vmem(queries.shape, BF16),
+        vmem(keys.shape, BF16),
+        vmem(values.shape, BF16),
+        vmem(out_grad.shape, BF16),
+        vmem(forget.shape, BF16),
+        vmem(inputs.shape, BF16),
+        vmem((8, 128), BF16),
+        pltpu.SemaphoreType.DMA((7,)),
         vmem((HEADS, 2, block, dk + dv), F32),
         vmem((HEADS, 2, block, dk + dv), F32),
         vmem((HEADS, 2, block, dk + dv), F32),
@@ -520,8 +654,8 @@
         vmem((rows_y, 8, 128), F32),
         vmem((8, 128), F32),
         vmem((HEADS, 8, 128), F32),
-        vmem((8, dv), F32),
-        vmem((rows_y, 8, dv), F32),
+        vmem((2, 128), F32),
+        vmem((rows_y, 2, 128), F32),
         vmem((2, 128), F32),
         vmem((count_dp, 2, 128), F32),
         vmem((2, 128), F32),
@@ -532,26 +666,42 @@
         pltpu.SemaphoreType.DMA((11, rows_y - 1)),
         pltpu.SemaphoreType.DMA((max(count_dp - 1, 1),)),
         pltpu.SemaphoreType.DMA((max(count_dp - 1, 1),)),
+        pltpu.SemaphoreType.DMA((1,)),
+        pltpu.SemaphoreType.DMA((rows_y,)),
+        pltpu.SemaphoreType.DMA((HEADS * rows_y - 1,)),
+        pltpu.SemaphoreType.DMA((HEADS,)),
+        pltpu.SemaphoreType.REGULAR,
     ]
     spec = pl.BlockSpec(memory_space=pltpu.VMEM)
+    hbm = pl.BlockSpec(memory_space=pltpu.HBM)
+    shapes = (
+        jax.ShapeDtypeStruct(queries.shape, BF16),
+        jax.ShapeDtypeStruct(keys.shape, BF16),
+        jax.ShapeDtypeStruct(values.shape, BF16),
+        jax.ShapeDtypeStruct(forget.shape, F32),
+        jax.ShapeDtypeStruct(inputs.shape, F32),
+        jax.ShapeDtypeStruct((8, 128), F32),
+    )
     outs = pl.pallas_call(
         functools.partial(kernel, rows_y, count_dp),
-        out_shape=(
-            jax.ShapeDtypeStruct(queries.shape, BF16),
-            jax.ShapeDtypeStruct(keys.shape, BF16),
-            jax.ShapeDtypeStruct(values.shape, BF16),
-            jax.ShapeDtypeStruct(forget.shape, F32),
-            jax.ShapeDtypeStruct(inputs.shape, F32),
-            jax.ShapeDtypeStruct((8, 128), F32),
-        ),
-        in_specs=[spec] * 7,
+        out_shape=shapes,
+        in_specs=[hbm] * 7,
         out_specs=(spec,) * 6,
         scratch_shapes=scratch,
         compiler_params=pltpu.CompilerParams(
             collective_id=0, has_side_effects=True, vmem_limit_bytes=48 * 1024 * 1024
         ),
         name="mlstm_back",
-    )(queries, keys, values, out_grad, forget, inputs, gain.reshape(HEADS, -1))
+    )(*[pltpu.with_memory_space_constraint(a, pltpu.HBM) for a in (queries, keys, values, out_grad, forget, inputs, gain.reshape(8, 128))])
+    outs = pl.pallas_call(
+        store,
+        out_shape=shapes,
+        in_specs=[spec] * 6,
+        out_specs=(hbm,) * 6,
+        scratch_shapes=[pltpu.SemaphoreType.DMA((6,))],
+        compiler_params=pltpu.CompilerParams(vmem_limit_bytes=1048576),
+        name="store",
+    )(*outs)
     return outs[:5] + (outs[5].reshape(-1),)
 
 

time: 79.9 us -> 68.6 us (0.86)
  local copies, waits for them, and re-layouts: 8.2 us -> 0 us
  Pallas kernels: 70.3 us -> 67.8 us
    unnamed x18 -> x0, local copies, waits for them, and re-layouts: 7.5 us -> none
    pallas_call x1 -> x2, Pallas kernels: 70.3 us -> 67.8 us  [the longest x1 66.9 us: shards(): pl.pallas_call(functools.partial(kernel, rows_y, count_dp), out_shape=sha...]
where the time goes in v2:
time: 68.6 us; the launch traced here: 68.4 us
  Pallas kernels  67.8 us (99%)
    pallas_call x1, Pallas kernels, shards(): pl.pallas_call(functools.partial(kernel, rows_y, count_dp), out_shape=sha...  66.9 us

profile of v2, /device:TPU:6, one launch (start us, length us, event | category | flops | bytes accessed | tf_op | source)
XLA Modules:
  0.0 68.4 jit_solution(11141175299580879683)
XLA Ops:
  0.6 66.9 %mlstm_back.1 = (bf16[1,2,64,512]{3,2,1,0:T(8,128)(2,1)S(1)}, bf16[1,2,64,512]{3,2,1,0:T(8,128)(2,1)S(1)}, bf16[1,2,64,1024]{3,2,1,0:T(8,128)(2,1)S(1)}, f32[1,2...) custom-call(bf16[1,2,64,512]{3,2,1,0:T(8,128)(2,1)} %q_hbm.1, ...), custom_call_target="tpu_custom_call" | custom-call | tf_op jit(solution)/shard_map/mlstm_back/pallas_call | solution.py:685
  67.6 0.9 %store.1 = (bf16[1,2,64,512]{3,2,1,0:T(8,128)(2,1)}, bf16[1,2,64,512]{3,2,1,0:T(8,128)(2,1)}, bf16[1,2,64,1024]{3,2,1,0:T(8,128)(2,1)}, f32[1,2,4,64]{3,2,1,0:T(...) custom-call(bf16[1,2,64,512]{3,2,1,0:T(8,128)(2,1)S(1)} %get-tuple-element.18.refs_0_, ...), custom_call_target="tpu_custom_call" | custom-call | tf_op jit(solution)/shard_map/store/pallas_call | solution.py:696

commit v3 on v2

--- a/solution.py
+++ b/solution.py
@@ -103,10 +103,10 @@
         pltpu.make_async_copy(src, dst, in_sem.at[number])
         for number, (src, dst) in enumerate(
             [
+                (k_hbm, k_ref),
+                (v_hbm, v_ref),
                 (f_hbm, f_ref),
                 (i_hbm, i_ref),
-                (k_hbm, k_ref),
-                (v_hbm, v_ref),
                 (q_hbm, q_ref),
                 (g_hbm, g_ref),
                 (gain_hbm, gain_ref),
@@ -193,10 +193,39 @@
             signal(barrier, to_d(step))
 
 
+    inputs[0].wait()
+    inputs[1].wait()
+
+    def widen(leg):
+        for head in range(HEADS):
+            s_kv[head, leg, :, :dk] = k_ref[0, leg, :, head * dk : (head + 1) * dk].astype(F32)
+            s_kv[head, leg, :, dk:] = v_ref[0, leg, :, head * dv : (head + 1) * dv].astype(F32)
+
+    def send_kv(leg):
+        return x_send(1 + leg, lambda step: s_kv.at[x_peer(step), leg], r_kv.at[my_x, leg])
+
+    widen(0)
+    @pl.when(jnp.logical_not(is_gate))
+    def _():
+        pl.semaphore_wait(barrier, plane)
+
+        @pl.when((my_y < HEADS) & (my_x == lax.rem(my_y + 1, HEADS)))
+        def _():
+            signal(ready, {"ctx": my_y * HEADS + my_y})
+
+        @pl.when(my_y == lax.rem(my_x + 1, rows_y))
+        def _():
+            signal(ready, {"ctx": my_x * HEADS + my_x})
+
+    @pl.when(is_gate)
+    def _():
+        pl.semaphore_wait(ready, 2)
+
+    kv_in = [send_kv(0)]
     lane8 = lax.broadcasted_iota(jnp.int32, (8, 128), 1)
     row8 = lax.broadcasted_iota(jnp.int32, (8, 128), 0)
-    inputs[0].wait()
-    inputs[1].wait()
+    inputs[2].wait()
+    inputs[3].wait()
     forget = jnp.concatenate([f_ref[0, 0], f_ref[0, 1]], axis=0).astype(F32)
     ingate_l = jnp.concatenate([i_ref[0, 0], i_ref[0, 1]], axis=0).astype(F32)
     logsig = -jnp.log1p(jnp.exp(-forget))
@@ -212,34 +241,9 @@
     s_gate[...] = cum
     r_gate[my_x] = cum
 
-    inputs[2].wait()
-    inputs[3].wait()
-    for leg in range(2):
-        for head in range(HEADS):
-            s_kv[head, leg, :, :dk] = k_ref[0, leg, :, head * dk : (head + 1) * dk].astype(F32)
-            s_kv[head, leg, :, dk:] = v_ref[0, leg, :, head * dv : (head + 1) * dv].astype(F32)
-
-    @pl.when(jnp.logical_not(is_gate))
-    def _():
-        pl.semaphore_wait(barrier, plane)
-
-        @pl.when((my_y < HEADS) & (my_x == lax.rem(my_y + 1, HEADS)))
-        def _():
-            signal(ready, {"ctx": my_y * HEADS + my_y})
-
-        @pl.when(my_y == lax.rem(my_x + 1, rows_y))
-        def _():
-            signal(ready, {"ctx": my_x * HEADS + my_x})
-
-    @pl.when(is_gate)
-    def _():
-        pl.semaphore_wait(ready, 2)
-
     gate_in = x_send(0, lambda step: s_gate, r_gate.at[my_x])
-    kv_in = [
-        x_send(1 + leg, lambda step, leg=leg: s_kv.at[x_peer(step), leg], r_kv.at[my_x, leg])
-        for leg in range(2)
-    ]
+    widen(1)
+    kv_in.append(send_kv(1))
     for copy in inputs[4:]:
         copy.wait()
     for leg in range(2):
@@ -313,13 +317,15 @@
         for row in path:
             s_state[phase, leg, row] = state
             state = twice(r_fade[row, leg : leg + 1, :]) * state + slices[phase, leg, row]
+        return state
+
+    def return_rows(phase, leg):
         r_state[phase, leg, my_y] = s_state[phase, leg, my_y]
-        copies = y_send(
+        return y_send(
             4 + 4 * phase + 2 * leg,
             lambda step: s_state.at[phase, leg, y_peer(step)],
             r_state.at[phase, leg, my_y],
         )
-        return state, copies
 
     slices_in = [[None, None], [None, None]]
     states_in = [[None, None], [None, None]]
@@ -333,8 +339,8 @@
 
     qg_in = [
         x_send(3 + leg, lambda step, leg=leg: s_qg.at[x_peer(step), leg], r_qg.at[my_x, leg])
-        for leg in range(2)
-    ]
+        for leg in (1, 0)
+    ][::-1]
 
     row_id = lax.broadcasted_iota(jnp.int32, (block, block), 0)
     col_id = lax.broadcasted_iota(jnp.int32, (block, block), 1)
@@ -344,11 +350,13 @@
     upward = list(range(rows_y))
     zero_state = jnp.zeros((part, dv), F32)
     arrive(slices_in[0][0])
-    through, states_in[0][0] = scan_rows(0, 0, upward, zero_state)
+    through = scan_rows(0, 0, upward, zero_state)
     arrive(slices_in[0][1])
-    _, states_in[0][1] = scan_rows(0, 1, upward[::-1], through)
-
-    for leg in range(2):
+    scan_rows(0, 1, upward[::-1], through)
+    states_in[0][1] = return_rows(0, 1)
+    states_in[0][0] = return_rows(0, 0)
+
+    for leg in (1, 0):
         arrive(qg_in[leg])
         for source in range(HEADS):
             index = leg * HEADS + source
@@ -362,6 +370,22 @@
             mix_b[index] = mix
             hidden_s[index] = dot(mix, value_of(leg, source), 0, 0)
 
+    def remote(src, dst, ss, rs, where):
+        return pltpu.make_async_remote_copy(
+            src_ref=src, dst_ref=dst, send_sem=ss, recv_sem=rs, device_id=where, device_id_type=MESH
+        )
+
+    def gain1():
+        gate = {"ctx": my_x * HEADS + my_x}
+        return remote(s_g1, r_g1.at[my_y], g1_ss.at[0], g1_rs.at[my_y], gate)
+
+    def gain2(step):
+        return remote(s_g2, r_g2.at[my_dp], d_ss.at[step - 1], d_rs.at[step - 1], to_d(step))
+
+    def gain3(step):
+        where = {"ctx": lax.rem(me + step, HEADS * rows_y)}
+        return remote(s_g3, r_g3.at[my_x], g3_ss.at[step - 1], g3_rs.at[my_x], where)
+
     lane_b = lax.broadcasted_iota(jnp.int32, (block, 128), 1)
     gain_all = gain_ref[...].astype(F32)
     head_id = lax.broadcasted_iota(jnp.int32, gain_all.shape, 0)
@@ -374,7 +398,7 @@
     )
     gain_sum = jnp.zeros((8, dv), F32)
     ghh = jnp.zeros((block, 128), F32)
-    for leg in range(2):
+    for leg in (1, 0):
         arrive(states_in[0][leg])
         state = r_state[0, leg].reshape(dk, dv)
         for source in order[0][leg]:
@@ -400,34 +424,18 @@
                 lane_b == index, jnp.sum(grad_hidden * hidden, axis=1, keepdims=True), ghh
             )
             state = fade_of(index) * state + writes[0, leg, source]
+        if leg == 0:
+            gain_sum = jnp.sum(gain_sum, axis=0, keepdims=True)
+            gain_sum = jnp.concatenate([gain_sum[:, :128], gain_sum[:, 128:]], axis=0)
+            s_g1[...] = gain_sum
+            r_g1[my_y] = gain_sum
+
+            @pl.when(jnp.logical_not(is_gate))
+            def _():
+                gain1().start()
+
+        slices_in[1][leg] = send_total(1, leg)
     ghh_cols[...] = ghh
-    slices_in[1][1] = send_total(1, 1)
-    slices_in[1][0] = send_total(1, 0)
-    gain_sum = jnp.sum(gain_sum, axis=0, keepdims=True)
-    gain_sum = jnp.concatenate([gain_sum[:, :128], gain_sum[:, 128:]], axis=0)
-    s_g1[...] = gain_sum
-    r_g1[my_y] = gain_sum
-
-    def remote(src, dst, ss, rs, where):
-        return pltpu.make_async_remote_copy(
-            src_ref=src, dst_ref=dst, send_sem=ss, recv_sem=rs, device_id=where, device_id_type=MESH
-        )
-
-    def gain1():
-        gate = {"ctx": my_x * HEADS + my_x}
-        return remote(s_g1, r_g1.at[my_y], g1_ss.at[0], g1_rs.at[my_y], gate)
-
-    def gain2(step):
-        return remote(s_g2, r_g2.at[my_dp], d_ss.at[step - 1], d_rs.at[step - 1], to_d(step))
-
-    def gain3(step):
-        where = {"ctx": lax.rem(me + step, HEADS * rows_y)}
-        return remote(s_g3, r_g3.at[my_x], g3_ss.at[step - 1], g3_rs.at[my_x], where)
-
-    @pl.when(jnp.logical_not(is_gate))
-    def _():
-        gain1().start()
-
     own_sum = jnp.zeros((block, 128), F32)
     grad_q_in = [None, None]
     for leg in (1, 0):
@@ -454,9 +462,8 @@
     own_cols[...] = own_sum
 
     arrive(slices_in[1][1])
-    through, states_in[1][1] = scan_rows(1, 1, upward, zero_state)
-    arrive(slices_in[1][0])
-    _, states_in[1][0] = scan_rows(1, 0, upward[::-1], through)
+    through = scan_rows(1, 1, upward, zero_state)
+    states_in[1][1] = return_rows(1, 1)
 
     @pl.when(is_gate)
     def _():
@@ -473,7 +480,14 @@
         for step in range(1, count_dp):
             gain2(step).start()
 
-
+    arrive(slices_in[1][0])
+    scan_rows(1, 0, upward[::-1], through)
+    states_in[1][0] = return_rows(1, 0)
+
+    for leg in (1, 0):
+        arrive(grad_q_in[leg])
+        for head in range(HEADS):
+            gq_ref[0, leg, :, head * dk : (head + 1) * dk] = r_q[head, leg].astype(BF16)
     own_sum = own_cols[...]
     out_in = [None, None]
     for leg in (1, 0):
@@ -515,6 +529,19 @@
     r_lift[my_y] = tile
     lift_in = y_send(1, lambda step: s_lift, r_lift.at[my_y])
 
+    @pl.when(is_gate)
+    def _():
+        for step in range(1, count_dp):
+            gain2(step).wait_recv()
+        gain_sum = r_g2[0]
+        for row in range(1, count_dp):
+            gain_sum = gain_sum + r_g2[row]
+        s_g3[...] = gain_sum
+        r_g3[my_x] = gain_sum
+        for step in range(1, HEADS * rows_y):
+            gain3(step).start()
+
+
     later_rows = [None] * 8
     zero_row = jnp.zeros((1, 128), F32)
     run = zero_row
@@ -545,10 +572,6 @@
     fin_in = x_send(9, lambda step: s_fin, r_fin.at[my_x])
 
     for leg in (1, 0):
-        arrive(grad_q_in[leg])
-        for head in range(HEADS):
-            gq_ref[0, leg, :, head * dk : (head + 1) * dk] = r_q[head, leg].astype(BF16)
-    for leg in (1, 0):
         arrive(out_in[leg])
         for head in range(HEADS):
             gk_ref[0, leg, :, head * dk : (head + 1) * dk] = r_out[head, leg, :, :dk].astype(BF16)
@@ -561,18 +584,6 @@
         slope = 1.0 / (1.0 + jnp.exp(f_ref[0, leg].astype(F32)))
         gi_ref[0, leg] = rows[:, :block]
         gf_ref[0, leg] = rows[:, block:] * slope
-
-    @pl.when(is_gate)
-    def _():
-        for step in range(1, count_dp):
-            gain2(step).wait_recv()
-        gain_sum = r_g2[0]
-        for row in range(1, count_dp):
-            gain_sum = gain_sum + r_g2[row]
-        s_g3[...] = gain_sum
-        r_g3[my_x] = gain_sum
-        for step in range(1, HEADS * rows_y):
-            gain3(step).start()
 
     for copy in started:
         copy.wait_send()

time: 68.6 us -> 63.9 us (0.931)
  Pallas kernels: 67.8 us -> 63.2 us
    pallas_call x1, Pallas kernels: 66.9 us -> 62.3 us  [shards(): pl.pallas_call(functools.partial(kernel, rows_y, count_dp), out_shape=sha...]
where the time goes in v3:
time: 63.9 us; the launch traced here: 63.8 us
  Pallas kernels  63.2 us (99%)
  between operations  0.64 us (1%)
    pallas_call x1, Pallas kernels, shards(): pl.pallas_call(functools.partial(kernel, rows_y, count_dp), out_shape=sha...  62.3 us

profile of v3, /device:TPU:6, one launch (start us, length us, event | category | flops | bytes accessed | tf_op | source)
XLA Modules:
  0.0 63.8 jit_solution(313775802130782339)
XLA Ops:
  0.6 62.3 %mlstm_back.1 = (bf16[1,2,64,512]{3,2,1,0:T(8,128)(2,1)S(1)}, bf16[1,2,64,512]{3,2,1,0:T(8,128)(2,1)S(1)}, bf16[1,2,64,1024]{3,2,1,0:T(8,128)(2,1)S(1)}, f32[1,2...) custom-call(bf16[1,2,64,512]{3,2,1,0:T(8,128)(2,1)} %q_hbm.1, ...), custom_call_target="tpu_custom_call" | custom-call | tf_op jit(solution)/shard_map/mlstm_back/pallas_call | solution.py:696
  62.9 0.9 %store.1 = (bf16[1,2,64,512]{3,2,1,0:T(8,128)(2,1)}, bf16[1,2,64,512]{3,2,1,0:T(8,128)(2,1)}, bf16[1,2,64,1024]{3,2,1,0:T(8,128)(2,1)}, f32[1,2,4,64]{3,2,1,0:T(...) custom-call(bf16[1,2,64,512]{3,2,1,0:T(8,128)(2,1)S(1)} %get-tuple-element.18.refs_0_, ...), custom_call_target="tpu_custom_call" | custom-call | tf_op jit(solution)/shard_map/store/pallas_call | solution.py:707

commit v4 on v3

--- a/solution.py
+++ b/solution.py
@@ -18,6 +18,10 @@
     return lax.dot_general(
         left, right, (((left_dim,), (right_dim,)), ((), ())), preferred_element_type=F32
     )
+
+
+def far_first(count):
+    return sorted(range(1, count), key=lambda step: -min(step, count - step))
 
 
 def twice(row):
@@ -161,7 +165,7 @@
     def y_send(kind, source, target):
         return [
             send(source(step), target, y_ss.at[kind, step - 1], y_rs.at[kind, step - 1], to_y(step))
-            for step in range(1, rows_y)
+            for step in far_first(rows_y)
         ]
 
     def arrive(copies):

time: 63.9 us -> 61.6 us (0.964); the launches traced: 63.8 us -> 60.8 us
  Pallas kernels: 63.2 us -> 60.2 us
    pallas_call x1, Pallas kernels: 62.3 us -> 59.3 us  [shards(): pl.pallas_call(functools.partial(kernel, rows_y, count_dp), out_shape=sha...]
where the time goes in v4:
time: 61.6 us; the launch traced here: 60.8 us
  Pallas kernels  60.2 us (98%)
  between operations  0.64 us (1%)
    pallas_call x1, Pallas kernels, shards(): pl.pallas_call(functools.partial(kernel, rows_y, count_dp), out_shape=sha...  59.3 us

profile of v4, /device:TPU:6, one launch (start us, length us, event | category | flops | bytes accessed | tf_op | source)
XLA Modules:
  0.0 60.8 jit_solution(10872622063677938809)
XLA Ops:
  0.6 59.3 %mlstm_back.1 = (bf16[1,2,64,512]{3,2,1,0:T(8,128)(2,1)S(1)}, bf16[1,2,64,512]{3,2,1,0:T(8,128)(2,1)S(1)}, bf16[1,2,64,1024]{3,2,1,0:T(8,128)(2,1)S(1)}, f32[1,2...) custom-call(bf16[1,2,64,512]{3,2,1,0:T(8,128)(2,1)} %q_hbm.1, ...), custom_call_target="tpu_custom_call" | custom-call | tf_op jit(solution)/shard_map/mlstm_back/pallas_call | solution.py:700
  60.0 0.9 %store.1 = (bf16[1,2,64,512]{3,2,1,0:T(8,128)(2,1)}, bf16[1,2,64,512]{3,2,1,0:T(8,128)(2,1)}, bf16[1,2,64,1024]{3,2,1,0:T(8,128)(2,1)}, f32[1,2,4,64]{3,2,1,0:T(...) custom-call(bf16[1,2,64,512]{3,2,1,0:T(8,128)(2,1)S(1)} %get-tuple-element.18.refs_0_, ...), custom_call_target="tpu_custom_call" | custom-call | tf_op jit(solution)/shard_map/store/pallas_call | solution.py:711

commit v5 on v4

--- a/solution.py
+++ b/solution.py
@@ -107,10 +107,12 @@
         pltpu.make_async_copy(src, dst, in_sem.at[number])
         for number, (src, dst) in enumerate(
             [
-                (k_hbm, k_ref),
-                (v_hbm, v_ref),
+                (k_hbm.at[:, 0], k_ref.at[:, 0]),
+                (v_hbm.at[:, 0], v_ref.at[:, 0]),
                 (f_hbm, f_ref),
                 (i_hbm, i_ref),
+                (k_hbm.at[:, 1], k_ref.at[:, 1]),
+                (v_hbm.at[:, 1], v_ref.at[:, 1]),
                 (q_hbm, q_ref),
                 (g_hbm, g_ref),
                 (gain_hbm, gain_ref),
@@ -246,9 +248,11 @@
     r_gate[my_x] = cum
 
     gate_in = x_send(0, lambda step: s_gate, r_gate.at[my_x])
+    inputs[4].wait()
+    inputs[5].wait()
     widen(1)
     kv_in.append(send_kv(1))
-    for copy in inputs[4:]:
+    for copy in inputs[6:]:
         copy.wait()
     for leg in range(2):
         r_kv[my_x, leg] = s_kv[my_x, leg]
@@ -481,7 +485,7 @@
         r_g2[my_dp] = gain_sum
         if count_dp > 1:
             pl.semaphore_wait(barrier, count_dp - 1)
-        for step in range(1, count_dp):
+        for step in far_first(count_dp):
             gain2(step).start()
 
     arrive(slices_in[1][0])
@@ -542,7 +546,7 @@
             gain_sum = gain_sum + r_g2[row]
         s_g3[...] = gain_sum
         r_g3[my_x] = gain_sum
-        for step in range(1, HEADS * rows_y):
+        for step in far_first(HEADS * rows_y):
             gain3(step).start()
 
 
@@ -635,7 +639,7 @@
         vmem(forget.shape, BF16),
         vmem(inputs.shape, BF16),
         vmem((8, 128), BF16),
-        pltpu.SemaphoreType.DMA((7,)),
+        pltpu.SemaphoreType.DMA((9,)),
         vmem((HEADS, 2, block, dk + dv), F32),
         vmem((HEADS, 2, block, dk + dv), F32),
         vmem((HEADS, 2, block, dk + dv), F32),

time: 61.6 us -> 61.3 us (level)
  no operation moved by 1% of the time
where the time goes in v5:
time: 61.3 us; the launch traced here: 60.3 us
  Pallas kernels  59.7 us (97%)
  between operations  0.64 us (1%)
    pallas_call x1, Pallas kernels, shards(): pl.pallas_call(functools.partial(kernel, rows_y, count_dp), out_shape=sha...  58.9 us

profile of v5, /device:TPU:6, one launch (start us, length us, event | category | flops | bytes accessed | tf_op | source)
XLA Modules:
  0.0 60.3 jit_solution(16953538774732409084)
XLA Ops:
  0.6 58.9 %mlstm_back.1 = (bf16[1,2,64,512]{3,2,1,0:T(8,128)(2,1)S(1)}, bf16[1,2,64,512]{3,2,1,0:T(8,128)(2,1)S(1)}, bf16[1,2,64,1024]{3,2,1,0:T(8,128)(2,1)S(1)}, f32[1,2...) custom-call(bf16[1,2,64,512]{3,2,1,0:T(8,128)(2,1)} %q_hbm.1, ...), custom_call_target="tpu_custom_call" | custom-call | tf_op jit(solution)/shard_map/mlstm_back/pallas_call | solution.py:704
  59.5 0.9 %store.1 = (bf16[1,2,64,512]{3,2,1,0:T(8,128)(2,1)}, bf16[1,2,64,512]{3,2,1,0:T(8,128)(2,1)}, bf16[1,2,64,1024]{3,2,1,0:T(8,128)(2,1)}, f32[1,2,4,64]{3,2,1,0:T(...) custom-call(bf16[1,2,64,512]{3,2,1,0:T(8,128)(2,1)S(1)} %get-tuple-element.18.refs_0_, ...), custom_call_target="tpu_custom_call" | custom-call | tf_op jit(solution)/shard_map/store/pallas_call | solution.py:715
